TPU v7x, 128 devices: a whole 4x4x4 slice. The times are simulated.
128 devices in a mesh: dp: 8 (over x, core), fsdp: 16 (over z, y).
Axes of the slice: x: 4, y: 4, z: 4, core: 2. Of those that a mesh axis runs over, the one named last changes fastest.
Arguments:
- q_inputs: bfloat16 [131072, 768], P(('dp', 'fsdp')), may hold values from -6 to 6
- q_grads: bfloat16 [131072, 6144], P(('dp', 'fsdp')), may hold values from -0.15625 to 0.15625
- k_inputs: bfloat16 [131072, 512], P(('dp', 'fsdp')), may hold values from -6 to 6
- k_grads: bfloat16 [131072, 4096], P(('dp', 'fsdp')), may hold values from -0.15625 to 0.15625
- q_master: float32 [6144, 768], P(('dp', 'fsdp')), may hold values from -3 to 3
- k_master: float32 [4096, 512], P(('dp', 'fsdp')), may hold values from -3 to 3
- q_momentum: float32 [6144, 768], P(('dp', 'fsdp')), may hold values from -25 to 25, as said below
- k_momentum: float32 [4096, 512], P(('dp', 'fsdp')), may hold values from -25 to 25, as said below
- logit_peaks: float32 [128, 32], P(('dp', 'fsdp')), may hold values from 10 to 500, as said below
- clip_flags: int32 [2, 32], replicated, may hold values 0 or 1
Outputs:
- new_q_master: float32 [6144, 768], P(('dp', 'fsdp'))
- new_k_master: float32 [4096, 512], P(('dp', 'fsdp'))
- new_q_momentum: float32 [6144, 768], P(('dp', 'fsdp'))
- new_k_momentum: float32 [4096, 512], P(('dp', 'fsdp'))
- q_weights: bfloat16 [6144, 768], P('dp')
- k_weights: bfloat16 [4096, 512], P('dp')
Inputs may be any that keep to these rules, and one draw needn't show every extreme that they name: `q_momentum`: the momenta are finite reals of mixed sign. `k_momentum`: the momenta are finite reals of mixed sign. `logit_peaks`: every entry is positive.
All inputs are finite; a program needn't handle non-finite values.
Results may differ from a plain program's by a relative error of at most 0.0004.
Values may be sent and summed in bfloat16 or wider, within the bound.
No kernel may reach another device: no remote copies, remote signals or barrier semaphores. Data moves between devices by JAX's collectives and lax.ppermute only.
A program may use at most 128 MiB of HBM per device.

v0:
```python
import math

import jax
import jax.numpy as jnp
from jax import lax
from jax.sharding import PartitionSpec as P

QNOPE = 128
QROPE = 64
NS_ITERS = 3


COEF_A = 3.4445
COEF_B = -4.775
COEF_C = 2.0315
MOMENTUM_RATE = 0.95
STEP_SIZE = 0.5
DECAY_RATE = 0.1
LOGIT_CAP = 100.0
NORM_EPS = 1e-07
HIGH = lax.Precision.HIGHEST


def hdot(first, second):
    return jnp.dot(first, second, precision=HIGH, preferred_element_type=jnp.float32)


def gram(current):
    return lax.dot_general(
        current,
        current,
        (((0,), (0,)), ((), ())),
        precision=HIGH,
        preferred_element_type=jnp.float32,
    )


def gram_pair(first, second):
    return lax.psum((gram(first), gram(second)), ("dp", "fsdp"))


def column_terms(grads, inputs):
    return lax.dot_general(
        grads, inputs, (((0,), (0,)), ((), ())), preferred_element_type=jnp.float32
    )


def newton_step(current, gram_sum):
    mixed = COEF_B * gram_sum + COEF_C * hdot(gram_sum, gram_sum)
    return COEF_A * current + hdot(current, mixed)


def row_factors(row_ids, head_span, nope_width, flags, ratio, root, heads):
    head_ids = row_ids // head_span
    is_nope = row_ids % head_span < nope_width
    chosen = flags == 1
    nope_value = jnp.where(chosen, root, 1.0)
    rope_value = jnp.where(chosen, ratio, 1.0)
    onehot = (head_ids[:, None] == lax.iota(jnp.int32, heads)[None, :]).astype(jnp.float32)
    values = jnp.where(is_nope[:, None], nope_value[None, :], rope_value[None, :])
    return jnp.sum(onehot * values, axis=1)


def body(
    q_inputs,
    q_grads,
    k_inputs,
    k_grads,
    q_master,
    k_master,
    q_momentum,
    k_momentum,
    logit_peaks,
    clip_flags,
):
    shards = lax.axis_size(("dp", "fsdp"))
    q_rows = q_master.shape[0]
    k_rows = k_master.shape[0]
    q_grad = lax.psum_scatter(
        column_terms(q_grads, q_inputs), ("dp", "fsdp"), scatter_dimension=0, tiled=True
    )
    k_grad = lax.psum_scatter(
        column_terms(k_grads, k_inputs), ("dp", "fsdp"), scatter_dimension=0, tiled=True
    )
    new_q_momentum = MOMENTUM_RATE * q_momentum + q_grad
    new_k_momentum = MOMENTUM_RATE * k_momentum + k_grad
    q_square, k_square = lax.psum(
        (jnp.sum(new_q_momentum * new_q_momentum), jnp.sum(new_k_momentum * new_k_momentum)),
        ("dp", "fsdp"),
    )
    q_iterate = new_q_momentum / (jnp.sqrt(q_square) + NORM_EPS)
    k_iterate = new_k_momentum / (jnp.sqrt(k_square) + NORM_EPS)
    q_gram, k_gram = gram_pair(q_iterate, k_iterate)
    for iteration in range(NS_ITERS):
        if iteration > 0:
            q_gram, k_gram = gram_pair(q_iterate, k_iterate)
        q_iterate = newton_step(q_iterate, q_gram)
        k_iterate = newton_step(k_iterate, k_gram)
    peaks = lax.pmax(logit_peaks[0], ("dp", "fsdp"))
    ratio = jnp.minimum(1.0, LOGIT_CAP / peaks)
    root = jnp.sqrt(ratio)
    heads = logit_peaks.shape[1]
    block = lax.axis_index(("dp", "fsdp"))
    q_ids = block * q_rows + lax.iota(jnp.int32, q_rows)
    k_ids = block * k_rows + lax.iota(jnp.int32, k_rows)
    q_factor = row_factors(q_ids, QNOPE + QROPE, QNOPE, clip_flags[0], ratio, root, heads)
    k_factor = row_factors(k_ids, QNOPE, QNOPE, clip_flags[1], ratio, root, heads)
    q_gain = 0.2 * math.sqrt(max(shards * q_rows, q_master.shape[1]))
    k_gain = 0.2 * math.sqrt(max(shards * k_rows, k_master.shape[1]))
    new_q_master = (q_master - STEP_SIZE * (q_gain * q_iterate + DECAY_RATE * q_master)) * q_factor[
        :, None
    ]
    new_k_master = (k_master - STEP_SIZE * (k_gain * k_iterate + DECAY_RATE * k_master)) * k_factor[
        :, None
    ]
    q_weights, k_weights = (
        lax.all_gather(new_q_master.astype(jnp.bfloat16), "fsdp", axis=0, tiled=True),
        lax.all_gather(new_k_master.astype(jnp.bfloat16), "fsdp", axis=0, tiled=True),
    )
    return (new_q_master, new_k_master, new_q_momentum, new_k_momentum, q_weights, k_weights)


def solution(mesh):
    placed = (
        P(("dp", "fsdp"), None),
        P(("dp", "fsdp"), None),
        P(("dp", "fsdp"), None),
        P(("dp", "fsdp"), None),
        P(("dp", "fsdp"), None),
        P(("dp", "fsdp"), None),
        P(("dp", "fsdp"), None),
        P(("dp", "fsdp"), None),
        P(("dp", "fsdp"), None),
        P(),
    )
    return jax.shard_map(
        body,
        mesh=mesh,
        in_specs=placed,
        out_specs=(
            P(("dp", "fsdp"), None),
            P(("dp", "fsdp"), None),
            P(("dp", "fsdp"), None),
            P(("dp", "fsdp"), None),
            P("dp", None),
            P("dp", None),
        ),
        check_vma=False,
    )
```

profile of v0, /device:TPU:0, one launch (start us, length us, event | category | flops | bytes accessed | tf_op | source)
XLA Modules:
  0.0 1550.2 jit_solution(17803236968363669840)
XLA Ops:
  7.2 11.7 fusion.69
  19.0 16.8 %fusion.63 = f32[6144,768]{1,0:T(8,128)} fusion(bf16[1024,6144]{1,0:T(8,128)(2,1)} %param.11, bf16[1024,768]{1,0:T(8,128)(2,1)S(1)} %copy-done), kind=kOutput, calls=%fused_computation.77 | convolution fusion | flops 9663676416 | bytes 33030144 | tf_op jit(solution)/shard_map/dot_general | solution.py:43
  35.8 644.0 %reduce-scatter.5.cloned.1.call-done = f32[32,512]{1,0:T(8,128)} async-done(((f32[4096,512]{1,0:T(8,128)}), f32[32,512]{1,0:T(8,128)}) %reduce-scatter.5.cloned.1.call-update) | async-done | bytes 65552 | tf_op jit(solution)/shard_map/reduce_scatter | solution.py:82
  679.8 1.5 multiply_reduce_fusion.1
  681.2 235.7 %reduce-scatter.3.cloned.1.call-done = f32[48,768]{1,0:T(8,128)} async-done(((f32[6144,768]{1,0:T(8,128)}), f32[48,768]{1,0:T(8,128)}) %reduce-scatter.3.cloned.1.call-update) | async-done | bytes 147472 | tf_op jit(solution)/shard_map/reduce_scatter | solution.py:79
  916.9 1.6 multiply_reduce_fusion
  918.5 73.6 %all-reduce = (f32[]{:T(128)}, f32[]{:T(128)}) all-reduce(f32[]{:T(128)} %get-tuple-element.18, f32[]{:T(128)} %get-tuple-element.16), channel_id=1, replica_groups=mesh['dp'=8,'fsdp'=16] {'dp','fsdp'}, use_global_device_ids=true, to_apply=%region_2.0 | all-reduce | flops 2 | bytes 16 | tf_op jit(solution)/shard_map/psum | solution.py:87
  993.5 2.0 fusion.51
  995.5 3.5 fusion.50
  999.1 148.5 %all-reduce.12.cloned.1.call-done = (f32[768,768]{1,0:T(8,128)}, f32[512,512]{1,0:T(8,128)}) async-done(((f32[768,768]{1,0:T(8,128)}, f32[512,512]{1,0:T(8,128)}), (f32[768,768]{1,0:T(8,128)}, f32[512,512]{1,0:T(8,128)})) %all-reduce.12.cloned.1.call-update) | async-done | bytes 3407888 | tf_op jit(solution)/shard_map/psum | solution.py:39
  1147.6 8.5 fusion.64
  1156.1 1.8 fusion.21
  1157.9 3.5 fusion.65
  1161.4 1.9 fusion.14
  1163.3 0.7 convolution_add_fusion.2
  1164.0 2.0 fusion.70
  1166.5 150.9 %all-reduce.10.cloned.1.call-done = (f32[768,768]{1,0:T(8,128)}, f32[512,512]{1,0:T(8,128)}) async-done(((f32[768,768]{1,0:T(8,128)}, f32[512,512]{1,0:T(8,128)}), (f32[768,768]{1,0:T(8,128)}, f32[512,512]{1,0:T(8,128)})) %all-reduce.10.cloned.1.call-update) | async-done | bytes 3407888 | tf_op jit(solution)/shard_map/psum | solution.py:39
  1317.4 8.5 fusion.66
  1325.9 1.8 fusion.24
  1327.7 3.5 fusion.67
  1331.2 1.9 fusion.13
  1333.8 2.0 fusion.71
  1335.9 64.9 %pmax.7 = f32[32]{0:T(128)S(1)} all-reduce(f32[32]{0:T(128)S(1)} %bitcast.38), channel_id=1, replica_groups=mesh['dp'=8,'fsdp'=16] {'dp','fsdp'}, use_global_device_ids=true, to_apply=%region_6.0 | all-reduce | flops 32 | bytes 256 | tf_op jit(solution)/shard_map/pmax | solution.py:99
  1401.0 86.3 %all-reduce.8.cloned.1.call-done = (f32[768,768]{1,0:T(8,128)}, f32[512,512]{1,0:T(8,128)}) async-done(((f32[768,768]{1,0:T(8,128)}, f32[512,512]{1,0:T(8,128)}), (f32[768,768]{1,0:T(8,128)}, f32[512,512]{1,0:T(8,128)})) %all-reduce.8.cloned.1.call-update) | async-done | bytes 3407888 | tf_op jit(solution)/shard_map/psum | solution.py:39
  1487.2 8.5 fusion.68
  1495.8 2.5 fusion.61
  1498.5 1.9 fusion.12
  1500.4 1.4 fusion.62
  1501.8 23.5 %all_gather.7 = bf16[512,512]{1,0:T(8,128)(2,1)S(1)} all-gather(bf16[32,512]{1,0:T(8,128)(2,1)S(1)} %get-tuple-element.25), channel_id=1, replica_groups=mesh['dp'=8,'fsdp'=16] {'fsdp'}, dimensions={0}, use_global_device_ids=true | all-gather | bytes 557056 | tf_op jit(solution)/shard_map/all_gather | solution.py:118
  1525.3 14.8 all-gather.2.cloned.1.call-done
  1540.1 2.4 copy.24
  1542.4 0.8 copy.25
  (53 shorter events, 1.9 us)
Async XLA Ops:
  7.2 11.8 copy-start
  7.2 672.6 %reduce-scatter.5.cloned.1.call-start = ((), (), s32[]{:S(2)}) async-start(), calls=%async_computation.3 | async-start | bytes 8454144 | tf_op jit(solution)/shard_map/reduce_scatter | solution.py:82
  18.9 898.0 %reduce-scatter.3.cloned.1.call-start = ((), (), s32[]{:S(2)}) async-start(), calls=%async_computation.2 | async-start | bytes 19021824 | tf_op jit(solution)/shard_map/reduce_scatter | solution.py:79
  35.7 644.0 %copy-start.12 = (f32[32,512]{1,0:T(8,128)S(1)}, f32[32,512]{1,0:T(8,128)}, u32[]{:S(2)}) copy-start(f32[32,512]{1,0:T(8,128)} %param.17) | copy-start | bytes 196612
  35.7 881.2 %copy-start.11 = (f32[48,768]{1,0:T(8,128)S(1)}, f32[48,768]{1,0:T(8,128)}, u32[]{:S(2)}) copy-start(f32[48,768]{1,0:T(8,128)} %param.16) | copy-start | bytes 442372
  35.8 1111.8 %all-reduce.12.cloned.1.call-start = ((), (), s32[]{:S(2)}) async-start(), calls=%async_computation.7 | async-start | bytes 6815744 | tf_op jit(solution)/shard_map/psum | solution.py:39
  681.2 482.0 %copy-start.9 = (f32[32,512]{1,0:T(8,128)}, f32[32,512]{1,0:T(8,128)S(1)}, u32[]{:S(2)}) copy-start(f32[32,512]{1,0:T(8,128)S(1)} %get-tuple-element.36) | copy-start | bytes 196612
  918.5 237.6 %copy-start.8 = (f32[48,768]{1,0:T(8,128)}, f32[48,768]{1,0:T(8,128)S(1)}, u32[]{:S(2)}) copy-start(f32[48,768]{1,0:T(8,128)S(1)} %get-tuple-element.35) | copy-start | bytes 442372
  999.0 318.4 %all-reduce.10.cloned.1.call-start = ((), (), s32[]{:S(2)}) async-start(), calls=%async_computation.6 | async-start | bytes 6815744 | tf_op jit(solution)/shard_map/psum | solution.py:39
  1147.6 8.5 copy-start.4
  1157.9 3.5 copy-start.6
  1166.0 321.2 %all-reduce.8.cloned.1.call-start = ((), (), s32[]{:S(2)}) async-start(), calls=%async_computation.5 | async-start | bytes 6815744 | tf_op jit(solution)/shard_map/psum | solution.py:39
  1317.4 8.5 copy-start.2
  1327.7 3.5 copy-start.7
  1333.8 2.1 copy-start.15
  1333.8 67.0 %copy-start.14 = (s32[2,32]{1,0:T(2,128)S(1)}, s32[2,32]{1,0:T(2,128)}, u32[]{:S(2)}) copy-start(s32[2,32]{1,0:T(2,128)} %param.19) | copy-start | bytes 772
  1335.8 204.2 %all-gather.2.cloned.1.call-start = ((), (), s32[]{:S(2)}) async-start(), calls=%async_computation.4 | async-start | bytes 1253376 | tf_op jit(solution)/shard_map/all_gather | solution.py:117
  1487.2 8.5 copy-start.3
  1487.2 8.5 copy-start.10
  1495.8 2.7 copy-start.5
  1498.2 2.2 copy-start.13
  1498.5 44.7 %copy-start.1 = (bf16[1024,768]{1,0:T(8,128)(2,1)S(1)}, bf16[1024,768]{1,0:T(8,128)(2,1)}, u32[]{:S(2)}) copy-start(bf16[1024,768]{1,0:T(8,128)(2,1)} %param.10) | copy-start | bytes 4718596
Sparse Core Ops, SparseCore 0:
  19.0 660.6 reduce-scatter.4
  685.1 231.8 reduce-scatter.2
  999.1 148.4 all-reduce.11
  1166.2 151.1 all-reduce.9
  1336.0 151.2 all-reduce.7
  1498.4 41.6 all-gather.1
where the time goes:
time: 1550 us
  waiting for transfers between devices  1280 us (83%)
  blocking collectives  162 us (10%)
  matrix products  84.8 us (5%)
  between operations  15.9 us (1%)
    reduce_scatter x1, waiting for transfers between devices, body(): lax.psum_scatter(column_terms(k_grads, k_inputs), ('dp', 'fsdp'), scatter...  644 us
    psum x3, waiting for transfers between devices, gram_pair(): return lax.psum((gram(first), gram(second)), ('dp', 'fsdp'))  386 us
    reduce_scatter x1, waiting for transfers between devices, body(): lax.psum_scatter(column_terms(q_grads, q_inputs), ('dp', 'fsdp'), scatter...  236 us
    psum x1, blocking collectives, body(): lax.psum((jnp.sum(new_q_momentum * new_q_momentum), jnp.sum(new_k_momentu...  73.6 us
    pmax x1, blocking collectives, body(): peaks = lax.pmax(logit_peaks[0], ('dp', 'fsdp'))  64.9 us
    dot_general x12, matrix products, hdot(): jnp.dot(first, second, precision=HIGH, preferred_element_type=jnp.float32)  39.9 us
  transfers between devices with their start and end apart: 6, of which 6 were waited for; matrix products, arithmetic and copies ran while one was open for 1% of the time, Pallas kernels for 0%

commit v1 on v0

--- a/solution.py
+++ b/solution.py
@@ -18,7 +18,7 @@
 DECAY_RATE = 0.1
 LOGIT_CAP = 100.0
 NORM_EPS = 1e-07
-HIGH = lax.Precision.HIGHEST
+HIGH = lax.Precision.HIGH
 
 
 def hdot(first, second):
@@ -45,9 +45,19 @@
     )
 
 
-def newton_step(current, gram_sum):
-    mixed = COEF_B * gram_sum + COEF_C * hdot(gram_sum, gram_sum)
-    return COEF_A * current + hdot(current, mixed)
+def orthogonalize(moment, moment_gram):
+    scale = 1.0 / (jnp.sqrt(jnp.trace(moment_gram)) + NORM_EPS)
+    current = moment * scale
+    gram_now = moment_gram * scale * scale
+    eye = jnp.eye(gram_now.shape[0], dtype=jnp.float32)
+    for iteration in range(NS_ITERS):
+        if iteration == NS_ITERS - 1:
+            inner = COEF_B * current + COEF_C * hdot(current, gram_now)
+            return COEF_A * current + hdot(inner, gram_now)
+        mixed = COEF_B * gram_now + COEF_C * hdot(gram_now, gram_now)
+        current = COEF_A * current + hdot(current, mixed)
+        step = COEF_A * eye + mixed
+        gram_now = hdot(hdot(gram_now, step), step)
 
 
 def row_factors(row_ids, head_span, nope_width, flags, ratio, root, heads):
@@ -76,27 +86,23 @@
     shards = lax.axis_size(("dp", "fsdp"))
     q_rows = q_master.shape[0]
     k_rows = k_master.shape[0]
-    q_grad = lax.psum_scatter(
-        column_terms(q_grads, q_inputs), ("dp", "fsdp"), scatter_dimension=0, tiled=True
-    )
-    k_grad = lax.psum_scatter(
-        column_terms(k_grads, k_inputs), ("dp", "fsdp"), scatter_dimension=0, tiled=True
-    )
+    q_terms = column_terms(q_grads, q_inputs).reshape(shards, q_rows, -1)
+    k_terms = column_terms(k_grads, k_inputs).reshape(shards, k_rows, -1)
+    k_terms = jnp.pad(k_terms, ((0, 0), (0, q_rows - k_rows), (0, 0)))
+    both = lax.psum_scatter(
+        jnp.concatenate((q_terms, k_terms), axis=2),
+        ("dp", "fsdp"),
+        scatter_dimension=0,
+        tiled=True,
+    )[0]
+    q_grad = both[:, : q_master.shape[1]]
+    k_grad = both[:k_rows, q_master.shape[1] :]
     new_q_momentum = MOMENTUM_RATE * q_momentum + q_grad
     new_k_momentum = MOMENTUM_RATE * k_momentum + k_grad
-    q_square, k_square = lax.psum(
-        (jnp.sum(new_q_momentum * new_q_momentum), jnp.sum(new_k_momentum * new_k_momentum)),
-        ("dp", "fsdp"),
-    )
-    q_iterate = new_q_momentum / (jnp.sqrt(q_square) + NORM_EPS)
-    k_iterate = new_k_momentum / (jnp.sqrt(k_square) + NORM_EPS)
-    q_gram, k_gram = gram_pair(q_iterate, k_iterate)
-    for iteration in range(NS_ITERS):
-        if iteration > 0:
-            q_gram, k_gram = gram_pair(q_iterate, k_iterate)
-        q_iterate = newton_step(q_iterate, q_gram)
-        k_iterate = newton_step(k_iterate, k_gram)
-    peaks = lax.pmax(logit_peaks[0], ("dp", "fsdp"))
+    q_gram, k_gram = gram_pair(new_q_momentum, new_k_momentum)
+    q_iterate = orthogonalize(new_q_momentum, q_gram)
+    k_iterate = orthogonalize(new_k_momentum, k_gram)
+    peaks = lax.pmax(lax.pmax(logit_peaks[0], "dp"), "fsdp")
     ratio = jnp.minimum(1.0, LOGIT_CAP / peaks)
     root = jnp.sqrt(ratio)
     heads = logit_peaks.shape[1]

time: 1550 us -> 567 us (0.37)
  waiting for transfers between devices: 1280 us -> 376 us
  blocking collectives: 162 us -> 74.1 us
    reduce_scatter x2 -> x1, waiting for transfers between devices: 880 us -> 267 us  [body(): lax.psum_scatter(jnp.concatenate((q_terms, k_terms), axis=2), ('dp', 'fsd...]
    psum x3 -> x1, waiting for transfers between devices: 386 us -> 97.6 us  [gram_pair(): return lax.psum((gram(first), gram(second)), ('dp', 'fsdp'))]
    psum x1 -> x0, blocking collectives: 73.6 us -> none  [body(): lax.psum((jnp.sum(new_q_momentum * new_q_momentum), jnp.sum(new_k_momentu...]
    pmax x1 -> x2, blocking collectives: 64.9 us -> 50.9 us  [body(): peaks = lax.pmax(lax.pmax(logit_peaks[0], 'dp'), 'fsdp')]
    dot_general x12 -> x20, matrix products: 39.9 us -> 41.6 us  [hdot(): jnp.dot(first, second, precision=HIGH, preferred_element_type=jnp.float32)]
  transfers between devices with their start and end apart: 6 -> 3, of which waited for: 6 -> 3; matrix products, arithmetic and copies ran while one was open for 1% -> 1% of each run, Pallas kernels for 0% -> 0%
where the time goes in v1:
time: 567 us; the launch traced here: 560 us
  waiting for transfers between devices  376 us (66%)
  blocking collectives  74.1 us (13%)
  matrix products  69.8 us (12%)
  other arithmetic  16.9 us (3%)
  between operations  16 us (3%)
  local copies, waits for them, and re-layouts  6.74 us (1%)
    reduce_scatter x1, waiting for transfers between devices, body(): lax.psum_scatter(jnp.concatenate((q_terms, k_terms), axis=2), ('dp', 'fsd...  267 us
    psum x1, waiting for transfers between devices, gram_pair(): return lax.psum((gram(first), gram(second)), ('dp', 'fsdp'))  97.6 us
    pmax x2, blocking collectives, body(): peaks = lax.pmax(lax.pmax(logit_peaks[0], 'dp'), 'fsdp')  50.9 us
    dot_general x20, matrix products, hdot(): jnp.dot(first, second, precision=HIGH, preferred_element_type=jnp.float32)  41.6 us
    dot_general x2, matrix products, column_terms(): lax.dot_general(grads, inputs, (((0,), (0,)), ((), ())), preferred_elemen...  24.1 us
    all_gather x1, blocking collectives, body(): lax.all_gather(new_k_master.astype(jnp.bfloat16), 'fsdp', axis=0, tiled=T...  23.2 us
    all_gather x1, waiting for transfers between devices, body(): lax.all_gather(new_q_master.astype(jnp.bfloat16), 'fsdp', axis=0, tiled=T...  11.9 us
  transfers between devices with their start and end apart: 3, of which 3 were waited for; matrix products, arithmetic and copies ran while one was open for 1% of the time, Pallas kernels for 0%

profile of v1, /device:TPU:0, one launch (start us, length us, event | category | flops | bytes accessed | tf_op | source)
XLA Modules:
  0.0 559.9 jit_solution(9992980084431107142)
XLA Ops:
  7.2 1.3 copy-done
  8.6 16.8 %fusion.68 = f32[6144,768]{1,0:T(8,128)} fusion(bf16[1024,6144]{1,0:T(8,128)(2,1)} %param.11, bf16[1024,768]{1,0:T(8,128)(2,1)S(1)} %copy-done), kind=kOutput, calls=%fused_computation.112 | convolution fusion | flops 9663676416 | bytes 33030144 | tf_op jit(solution)/shard_map/dot_general | solution.py:43
  25.4 7.3 %fusion.69 = f32[4096,512]{1,0:T(8,128)S(1)} fusion(bf16[1024,4096]{1,0:T(8,128)(2,1)} %param.13, bf16[1024,512]{1,0:T(8,128)(2,1)S(1)} %copy-done.18), kind=kOutput, calls=%fused_computation.113 | convolution fusion | flops 4294967296 | bytes 17825792 | tf_op jit(solution)/shard_map/dot_general | solution.py:43
  32.7 1.5 copy-done.2
  34.2 10.6 %select_maximum_fusion = f32[128,48,1280]{2,1,0:T(8,128)} fusion(f32[128,32,512]{2,1,0:T(8,128)S(1)} %bitcast.43, f32[128,48,768]{2,1,0:T(8,128)S(1)} %bitcast.42), kind=kLoop, calls=%fused_computation | loop fusion | flops 23592960 | bytes 58720256 | tf_op jit(solution)/shard_map/concatenate | solution.py:93
  44.9 266.5 %reduce-scatter.2.cloned.1.call-done = f32[1,48,1280]{2,1,0:T(8,128)} async-done(((f32[128,48,1280]{2,1,0:T(8,128)}), f32[1,48,1280]{2,1,0:T(8,128)}) %reduce-scatter.2.cloned.1.call-update) | async-done | bytes 245776 | tf_op jit(solution)/shard_map/reduce_scatter | solution.py:92
  311.4 0.9 slice_add_fusion
  312.4 2.5 fusion.70
  316.4 1.6 fusion.71
  318.1 12.8 %pmax.14 = f32[32]{0:T(128)S(1)} all-reduce(f32[32]{0:T(128)S(1)} %bitcast.46), channel_id=1, replica_groups=mesh['dp'=8,'fsdp'=16] {'dp'}, use_global_device_ids=true, to_apply=%region_3.4 | all-reduce | flops 32 | bytes 256 | tf_op jit(solution)/shard_map/pmax | solution.py:105
  330.9 38.1 %pmax.15 = f32[32]{0:T(128)S(1)} all-reduce(f32[32]{0:T(128)S(1)} %pmax.14), channel_id=1, replica_groups=mesh['dp'=8,'fsdp'=16] {'fsdp'}, use_global_device_ids=true, to_apply=%region_4.5 | all-reduce | flops 32 | bytes 256 | tf_op jit(solution)/shard_map/pmax | solution.py:105
  370.6 97.6 %all-reduce.4.cloned.1.call-done = (f32[768,768]{1,0:T(8,128)}, f32[512,512]{1,0:T(8,128)}) async-done(((f32[768,768]{1,0:T(8,128)}, f32[512,512]{1,0:T(8,128)}), (f32[768,768]{1,0:T(8,128)}, f32[512,512]{1,0:T(8,128)})) %all-reduce.4.cloned.1.call-update) | async-done | bytes 3407888 | tf_op jit(solution)/shard_map/psum | solution.py:39
  468.2 2.4 select_reduce_fusion
  471.3 6.5 %multiply_add_fusion.1 = f32[768,768]{1,0:T(8,128)S(1)} fusion(f32[768,768]{1,0:T(8,128)} %get-tuple-element.6, f32[]{:T(128)S(6)} %div.34), kind=kOutput, calls=%fused_computation.5 | convolution fusion | flops 2722037760 | bytes 4718596 | tf_op jit(solution)/shard_map/dot_general | solution.py:25
  477.8 4.5 fusion.1
  482.2 1.5 convolution_add_fusion.2
  485.2 3.2 fusion.6
  488.3 3.2 fusion.29
  491.5 3.3 fusion
  494.9 3.3 multiply_add_fusion
  498.2 3.1 fusion.3
  501.3 3.1 fusion.2
  505.4 0.9 fusion.20
  506.3 1.6 fusion.66
  508.4 1.3 fusion.30
  509.7 1.0 fusion.5
  511.1 1.0 fusion.32
  512.1 1.0 fusion.31
  513.6 1.0 fusion.67
  514.6 23.2 %all_gather.7 = bf16[512,512]{1,0:T(8,128)(2,1)S(1)} all-gather(bf16[32,512]{1,0:T(8,128)(2,1)S(1)} %get-tuple-element.15), channel_id=1, replica_groups=mesh['dp'=8,'fsdp'=16] {'fsdp'}, dimensions={0}, use_global_device_ids=true | all-gather | bytes 557056 | tf_op jit(solution)/shard_map/all_gather | solution.py:124
  537.8 11.9 %all-gather.2.cloned.1.call-done = bf16[768,768]{1,0:T(8,128)(2,1)} async-done(((bf16[48,768]{1,0:T(8,128)(2,1)}), bf16[768,768]{1,0:T(8,128)(2,1)}) %all-gather.2.cloned.1.call-update) | async-done | bytes 1179664 | tf_op jit(solution)/shard_map/all_gather | solution.py:123
  549.8 2.4 copy.20
  (59 shorter events, 6.8 us)
Async XLA Ops:
  7.2 1.4 copy-start
  7.2 18.2 %copy-start.18 = (bf16[1024,512]{1,0:T(8,128)(2,1)S(1)}, bf16[1024,512]{1,0:T(8,128)(2,1)}, u32[]{:S(2)}) copy-start(bf16[1024,512]{1,0:T(8,128)(2,1)} %param.12) | copy-start | bytes 3145732
  7.2 304.2 %reduce-scatter.2.cloned.1.call-start = ((), (), s32[]{:S(2)}) async-start(), calls=%async_computation.1 | async-start | bytes 31703040 | tf_op jit(solution)/shard_map/reduce_scatter | solution.py:92
  25.4 8.8 %copy-start.2 = (f32[6144,768]{1,0:T(8,128)S(1)}, f32[6144,768]{1,0:T(8,128)}, u32[]{:S(2)}) copy-start(f32[6144,768]{1,0:T(8,128)} %fusion.68) | copy-start | bytes 56623108
  44.8 266.6 %copy-start.12 = (f32[48,768]{1,0:T(8,128)S(1)}, f32[48,768]{1,0:T(8,128)}, u32[]{:S(2)}) copy-start(f32[48,768]{1,0:T(8,128)} %param.16) | copy-start | bytes 442372
  44.8 270.1 %copy-start.13 = (f32[32,512]{1,0:T(8,128)S(1)}, f32[32,512]{1,0:T(8,128)}, u32[]{:S(2)}) copy-start(f32[32,512]{1,0:T(8,128)} %param.17) | copy-start | bytes 196612
  44.8 423.3 %all-reduce.4.cloned.1.call-start = ((), (), s32[]{:S(2)}) async-start(), calls=%async_computation.3 | async-start | bytes 6815744 | tf_op jit(solution)/shard_map/psum | solution.py:39
  312.3 169.9 %copy-start.7 = (f32[48,768]{1,0:T(8,128)}, f32[48,768]{1,0:T(8,128)S(1)}, u32[]{:S(2)}) copy-start(f32[48,768]{1,0:T(8,128)S(1)} %slice_add_fusion) | copy-start | bytes 442372
  314.9 3.2 copy-start.19
  315.8 0.6 copy-start.8
  316.4 52.7 %copy-start.15 = (s32[2,32]{1,0:T(2,128)S(1)}, s32[2,32]{1,0:T(2,128)}, u32[]{:S(2)}) copy-start(s32[2,32]{1,0:T(2,128)} %param.19) | copy-start | bytes 772
  318.0 231.7 %all-gather.2.cloned.1.call-start = ((), (), s32[]{:S(2)}) async-start(), calls=%async_computation.2 | async-start | bytes 1253376 | tf_op jit(solution)/shard_map/all_gather | solution.py:123
  471.3 6.5 %copy-start.4 = (f32[768,768]{1,0:T(8,128)S(1)}, f32[768,768]{1,0:T(8,128)}, u32[]{:S(2)}) copy-start(f32[768,768]{1,0:T(8,128)} %get-tuple-element.6) | copy-start | bytes 7077892
  482.2 1.5 copy-start.6
  485.1 6.4 %copy-start.3 = (f32[768,768]{1,0:T(8,128)S(1)}, f32[768,768]{1,0:T(8,128)}, u32[]{:S(2)}) copy-start(f32[768,768]{1,0:T(8,128)} %fusion.1) | copy-start | bytes 7077892
  501.3 3.2 copy-start.10
  504.5 1.8 copy-start.11
  504.5 1.8 copy-start.17
  505.4 2.6 copy-start.9
  506.3 2.0 copy-start.5
  512.1 1.5 copy-start.14
  512.1 1.5 copy-start.16
  513.2 39.7 %copy-start.1 = (bf16[1024,768]{1,0:T(8,128)(2,1)S(1)}, bf16[1024,768]{1,0:T(8,128)(2,1)}, u32[]{:S(2)}) copy-start(bf16[1024,768]{1,0:T(8,128)(2,1)} %param.10) | copy-start | bytes 4718596
Sparse Core Ops, SparseCore 0:
  44.9 266.4 reduce-scatter.1
  318.1 149.9 all-reduce.3
  508.1 41.6 all-gather.1
